TPU v7x, 32 devices: a whole 2x2x4 slice. The times are simulated.
32 devices in a mesh: dp: 8 (over z, x), ctx: 4 (over y, core).
Axes of the slice: x: 2, y: 2, z: 4, core: 2. Of those that a mesh axis runs over, the one named last changes fastest.
Arguments:
- states: bfloat16 [32, 1024, 960], P('dp', 'ctx'), may hold values from -6 to 6
- teacher: bfloat16 [32, 1024, 960], P('dp', 'ctx'), may hold values from -6 to 6
- validity: int32 [32, 1024], P('dp', 'ctx'), may hold values from 0 to 1, as said below
- chosen: int32 [32, 1024], P('dp', 'ctx'), may hold values from 0 to 1, as said below
- attn_pack: bfloat16 [960, 2560], P(None, ('dp', 'ctx')), may hold values from -1 to 1
- gate_up: bfloat16 [960, 5120], P(None, ('dp', 'ctx')), may hold values from -0.1875 to 0.1875
- down_proj: bfloat16 [960, 2560], P(None, ('dp', 'ctx')), may hold values from -0.125 to 0.125
- norm_gains: float32 [2, 960], replicated, may hold values from 0.25 to 1.75
- router: float32 [960], replicated, may hold values from -0.12 to 0.12
Outputs:
- states_out: bfloat16 [32, 1024, 960], P('dp', 'ctx')
- mse_loss: float32 [], replicated
- states_grad: float32 [32, 1024, 960], P('dp', 'ctx')
- attn_pack_grad: float32 [960, 2560], P(None, ('dp', 'ctx'))
- gate_up_grad: float32 [960, 5120], P(None, ('dp', 'ctx'))
- down_proj_grad: float32 [960, 2560], P(None, ('dp', 'ctx'))
- norm_gains_grad: float32 [2, 960], replicated
- router_grad: float32 [960], replicated
Inputs may be any that keep to these rules, and one draw needn't show every extreme that they name: `validity`: the first token of every sequence is valid. `chosen`: each sequence has 640 or 641 selected tokens, the first token always among them.
All inputs are finite; a program needn't handle non-finite values.
Results may differ from a plain program's by a relative error of at most 0.012.
Values may be sent and summed in bfloat16 or wider, within the bound.
No kernel may reach another device: no remote copies, remote signals or barrier semaphores. Data moves between devices by JAX's collectives and lax.ppermute only.
A program may use at most 320 MiB of HBM per device.

v0:
```python
import jax
import jax.numpy as jnp
from jax import lax
from jax.sharding import PartitionSpec as P

D = 960
HEADS = 15
KV_HEADS = 5
HEAD = 64
FF = 2560
MICRO = 2
EPS = 1e-05
THETA = 10000.0


def shortened(x):
    return jax.tree.map(lambda a: a.astype(jnp.bfloat16) if a.dtype == jnp.float32 else a, x)


def rope_tables(positions):
    half_head = HEAD // 2
    freqs = THETA ** (-(jnp.arange(half_head).astype(jnp.float32) * 2.0 / HEAD))
    angles = positions.astype(jnp.float32)[:, None] * freqs[None, :]
    return (jnp.cos(angles)[:, None, :], jnp.sin(angles)[:, None, :])


def rotate(values, cosine, sine):
    half_head = HEAD // 2
    first = values[..., :half_head]
    second = values[..., half_head:]
    return jnp.concatenate(
        [first * cosine - second * sine, second * cosine + first * sine], axis=-1
    )


def rotate_back(values, cosine, sine):
    half_head = HEAD // 2
    first = values[..., :half_head]
    second = values[..., half_head:]
    return jnp.concatenate(
        [first * cosine + second * sine, second * cosine - first * sine], axis=-1
    )


def norm_back(grad_out, values, inv_rms, gain_row):
    scaled = grad_out * gain_row
    return inv_rms * scaled - values * inv_rms**3 * jnp.mean(
        scaled * values, axis=-1, keepdims=True
    )


def scores_of(queries, keys, allowed):
    scores = (
        jnp.einsum("bqgrh,bkgh->bgrqk", queries, keys, preferred_element_type=jnp.float32) * 0.125
    )
    return jnp.where(allowed, scores, -jnp.inf)


def over_rows(left, right):
    return lax.dot_general(
        left, right, (((0, 1), (0, 1)), ((), ())), preferred_element_type=jnp.float32
    )


def by_columns(left, right):
    return lax.dot_general(
        left, right, (((2,), (1,)), ((), ())), preferred_element_type=jnp.float32
    )


def on_device(states, teacher, validity, chosen, attn_pack, gate_up, down_proj, norm_gains, router):
    seq_count, block_rows, width = states.shape
    seq_micro = seq_count // MICRO
    ctx_count = lax.axis_size("ctx")
    dp_count = lax.axis_size("dp")
    ctx_spot = lax.axis_index("ctx")
    seq_length = block_rows * ctx_count
    qkv_cols = D + 2 * KV_HEADS * HEAD
    kv_width = KV_HEADS * HEAD
    per_kv = HEADS // KV_HEADS
    cosine, sine = rope_tables(ctx_spot * block_rows + jnp.arange(block_rows))
    early_block = jnp.arange(seq_length) // block_rows <= ctx_spot
    valid_all = validity.astype(jnp.float32)
    chosen_all = chosen.astype(jnp.float32)
    key_flags = (validity * chosen).astype(jnp.bfloat16)
    gain_one = norm_gains[0]
    gain_two = norm_gains[1]
    packs = (attn_pack, gate_up, down_proj)
    valid_total = lax.psum(jnp.sum(valid_all), ("dp", "ctx"))
    grad_attn = jnp.zeros((D, qkv_cols + D), jnp.float32)
    grad_gu = jnp.zeros((D, 2 * FF), jnp.float32)
    grad_down = jnp.zeros((D, FF), jnp.float32)
    grad_gain_one = jnp.zeros((D,), jnp.float32)
    grad_gain_two = jnp.zeros((D,), jnp.float32)
    grad_router = jnp.zeros((D,), jnp.float32)
    energy = jnp.zeros((), jnp.float32)
    out_parts = []
    input_grads = []
    for micro_index in range(MICRO):
        lower = micro_index * seq_micro
        upper = lower + seq_micro
        x_float = states[lower:upper].astype(jnp.float32)
        teacher_rows = teacher[lower:upper].astype(jnp.float32)
        valid_rows = valid_all[lower:upper]
        chosen_rows = chosen_all[lower:upper]
        fresh = (
            lax.all_gather(packs[0], ("dp", "ctx"), axis=1, tiled=True),
            lax.all_gather(packs[1], ("dp", "ctx"), axis=1, tiled=True),
            lax.all_gather(packs[2], ("dp", "ctx"), axis=1, tiled=True),
        )
        w_attn, w_gu, w_down = fresh
        inv_one = lax.rsqrt(jnp.mean(x_float * x_float, axis=-1, keepdims=True) + EPS)
        normed = (x_float * inv_one * gain_one).astype(jnp.bfloat16)
        mixed = jnp.dot(normed, w_attn[:, :qkv_cols], preferred_element_type=jnp.float32)
        queries = mixed[..., :D].reshape(seq_micro, block_rows, HEADS, HEAD)
        keys = mixed[..., D : D + kv_width].reshape(seq_micro, block_rows, KV_HEADS, HEAD)
        values_in = mixed[..., D + kv_width :].reshape(seq_micro, block_rows, KV_HEADS, HEAD)
        rot_queries = (
            rotate(queries, cosine, sine)
            .astype(jnp.bfloat16)
            .reshape(seq_micro, block_rows, KV_HEADS, per_kv, HEAD)
        )
        rot_keys = rotate(keys, cosine, sine).astype(jnp.bfloat16)
        value_low = values_in.astype(jnp.bfloat16)
        keys_all, values_all, flags_all = (
            lax.all_gather(rot_keys, "ctx", axis=1, tiled=True),
            lax.all_gather(value_low, "ctx", axis=1, tiled=True),
            lax.all_gather(key_flags[lower:upper], "ctx", axis=1, tiled=True),
        )
        allowed = (early_block[None, :] & (flags_all > 0.5))[:, None, None, None, :]
        scores = scores_of(rot_queries, keys_all, allowed)
        row_max = jnp.max(scores, axis=-1, keepdims=True)
        expd = jnp.exp(scores - row_max)
        row_total = jnp.sum(expd, axis=-1, keepdims=True)
        log_total = row_max + jnp.log(row_total)
        probs_low = (expd / row_total).astype(jnp.bfloat16)
        heads_out = jnp.einsum(
            "bgrqk,bkgh->bqgrh", probs_low, values_all, preferred_element_type=jnp.float32
        )
        heads_low = heads_out.reshape(seq_micro, block_rows, D).astype(jnp.bfloat16)
        attn_out = by_columns(heads_low, w_attn[:, qkv_cols:])
        inner = x_float + attn_out
        inv_two = lax.rsqrt(jnp.mean(inner * inner, axis=-1, keepdims=True) + EPS)
        normed_two = (inner * inv_two * gain_two).astype(jnp.bfloat16)
        gate_both = jnp.dot(normed_two, w_gu, preferred_element_type=jnp.float32)
        gate_part = gate_both[..., :FF]
        up_part = gate_both[..., FF:]
        gate_sig = jax.nn.sigmoid(gate_part)
        hidden = (gate_part * gate_sig * up_part).astype(jnp.bfloat16)
        ffn_out = by_columns(hidden, w_down)
        gate_prob = jax.nn.sigmoid(jnp.dot(x_float, router, precision=lax.Precision.HIGHEST))
        weight_mix = chosen_rows * gate_prob
        branch = attn_out + ffn_out
        result = x_float + weight_mix[..., None] * branch
        out_parts.append(result.astype(jnp.bfloat16))
        diff = valid_rows[..., None] * (result - teacher_rows)
        energy = energy + 0.5 * jnp.sum(diff * diff)
        w_attn, w_gu, w_down = (
            lax.all_gather(packs[0], ("dp", "ctx"), axis=1, tiled=True),
            lax.all_gather(packs[1], ("dp", "ctx"), axis=1, tiled=True),
            lax.all_gather(packs[2], ("dp", "ctx"), axis=1, tiled=True),
        )
        d_branch = weight_mix[..., None] * diff
        d_logit = chosen_rows * jnp.sum(diff * branch, axis=-1) * gate_prob * (1.0 - gate_prob)
        grad_router = grad_router + jnp.einsum(
            "bt,btd->d", d_logit, x_float, precision=lax.Precision.HIGHEST
        )
        d_states = diff + d_logit[..., None] * router
        d_ffn = d_branch.astype(jnp.bfloat16)
        d_hidden = jnp.dot(d_ffn, w_down, preferred_element_type=jnp.float32)
        grad_down = grad_down + over_rows(d_ffn, hidden)
        d_gate = d_hidden * up_part * gate_sig * (1.0 + gate_part * (1.0 - gate_sig))
        d_up = d_hidden * gate_part * gate_sig
        d_gu_low = jnp.concatenate([d_gate, d_up], axis=-1).astype(jnp.bfloat16)
        d_normed_two = by_columns(d_gu_low, w_gu)
        grad_gu = grad_gu + over_rows(normed_two, d_gu_low)
        grad_gain_two = grad_gain_two + jnp.sum(d_normed_two * inner * inv_two, axis=(0, 1))
        d_inner = norm_back(d_normed_two, inner, inv_two, gain_two)
        d_states = d_states + d_inner
        d_attn_low = (d_branch + d_inner).astype(jnp.bfloat16)
        d_heads = jnp.dot(d_attn_low, w_attn[:, qkv_cols:], preferred_element_type=jnp.float32)
        d_heads_low = d_heads.astype(jnp.bfloat16).reshape(
            seq_micro, block_rows, KV_HEADS, per_kv, HEAD
        )
        grad_out_proj = over_rows(d_attn_low, heads_low)
        probs = jnp.exp(scores_of(rot_queries, keys_all, allowed) - log_total)
        d_probs = jnp.einsum(
            "bqgrh,bkgh->bgrqk", d_heads_low, values_all, preferred_element_type=jnp.float32
        )
        d_scores = (probs * (d_probs - jnp.sum(probs * d_probs, axis=-1, keepdims=True))).astype(
            jnp.bfloat16
        )
        d_queries = (
            jnp.einsum("bgrqk,bkgh->bqgrh", d_scores, keys_all, preferred_element_type=jnp.float32)
            * 0.125
        )
        d_keys_all = (
            jnp.einsum(
                "bgrqk,bqgrh->bkgh", d_scores, rot_queries, preferred_element_type=jnp.float32
            )
            * 0.125
        )
        d_values_all = jnp.einsum(
            "bgrqk,bqgrh->bkgh",
            probs.astype(jnp.bfloat16),
            d_heads_low,
            preferred_element_type=jnp.float32,
        )
        d_keys, d_values = (
            lax.psum_scatter(
                d_keys_all.astype(jnp.bfloat16), "ctx", scatter_dimension=1, tiled=True
            ).astype(jnp.float32),
            lax.psum_scatter(
                d_values_all.astype(jnp.bfloat16), "ctx", scatter_dimension=1, tiled=True
            ).astype(jnp.float32),
        )
        d_queries = rotate_back(d_queries.reshape(seq_micro, block_rows, HEADS, HEAD), cosine, sine)
        d_keys = rotate_back(d_keys, cosine, sine)
        d_mixed = jnp.concatenate(
            [
                d_queries.reshape(seq_micro, block_rows, D),
                d_keys.reshape(seq_micro, block_rows, kv_width),
                d_values.reshape(seq_micro, block_rows, kv_width),
            ],
            axis=-1,
        ).astype(jnp.bfloat16)
        d_normed = by_columns(d_mixed, w_attn[:, :qkv_cols])
        grad_attn = grad_attn + jnp.concatenate([over_rows(normed, d_mixed), grad_out_proj], axis=1)
        grad_gain_one = grad_gain_one + jnp.sum(d_normed * x_float * inv_one, axis=(0, 1))
        d_states = d_states + norm_back(d_normed, x_float, inv_one, gain_one)
        input_grads.append(d_states)

    def owner_layout(grad_whole):
        return grad_whole.reshape(
            D, dp_count, ctx_count, grad_whole.shape[1] // (dp_count * ctx_count)
        )

    by_ctx = (
        lax.all_to_all(
            owner_layout(grad_attn).astype(jnp.bfloat16),
            "ctx",
            split_axis=2,
            concat_axis=2,
            tiled=True,
        ).astype(jnp.float32),
        lax.all_to_all(
            owner_layout(grad_gu).astype(jnp.bfloat16),
            "ctx",
            split_axis=2,
            concat_axis=2,
            tiled=True,
        ).astype(jnp.float32),
        lax.all_to_all(
            owner_layout(grad_down).astype(jnp.bfloat16),
            "ctx",
            split_axis=2,
            concat_axis=2,
            tiled=True,
        ).astype(jnp.float32),
    )
    attn_ctx, gu_ctx, down_ctx = [jnp.sum(piece, axis=2) for piece in by_ctx]
    by_dp = (
        lax.all_to_all(shortened(attn_ctx), "dp", split_axis=1, concat_axis=1, tiled=True).astype(
            attn_ctx.dtype
        ),
        lax.all_to_all(shortened(gu_ctx), "dp", split_axis=1, concat_axis=1, tiled=True).astype(
            gu_ctx.dtype
        ),
        lax.all_to_all(shortened(down_ctx), "dp", split_axis=1, concat_axis=1, tiled=True).astype(
            down_ctx.dtype
        ),
    )
    attn_grad_part, gu_grad_part, down_grad_part = [jnp.sum(piece, axis=1) for piece in by_dp]
    grad_gains = jnp.stack([grad_gain_one, grad_gain_two], axis=0)
    energy_all, gains_all, router_all = lax.psum((energy, grad_gains, grad_router), ("dp", "ctx"))
    mse_loss = 2.0 * energy_all / (valid_total * D)
    return (
        jnp.concatenate(out_parts, axis=0),
        mse_loss,
        jnp.concatenate(input_grads, axis=0),
        attn_grad_part,
        gu_grad_part,
        down_grad_part,
        gains_all,
        router_all,
    )


def solution(mesh):
    placed = (
        P("dp", "ctx", None),
        P("dp", "ctx", None),
        P("dp", "ctx"),
        P("dp", "ctx"),
        P(None, ("dp", "ctx")),
        P(None, ("dp", "ctx")),
        P(None, ("dp", "ctx")),
        P(),
        P(),
    )
    return jax.shard_map(
        on_device,
        mesh=mesh,
        in_specs=placed,
        out_specs=(
            P("dp", "ctx", None),
            P(),
            P("dp", "ctx", None),
            P(None, ("dp", "ctx")),
            P(None, ("dp", "ctx")),
            P(None, ("dp", "ctx")),
            P(),
            P(),
        ),
        check_vma=False,
    )
```

profile of v0, /device:TPU:0, one launch (start us, length us, event | category | flops | bytes accessed | tf_op | source)
XLA Modules:
  0.0 1026.9 jit_solution(13568377429993740406)
XLA Ops:
  10.8 68.1 %all-gather.8.cloned.1.call-done = bf16[960,2560]{0,1:T(8,128)(2,1)} async-done(((bf16[960,80]{0,1:T(8,128)(2,1)}), bf16[960,2560]{0,1:T(8,128)(2,1)}) %all-gather.8.cloned.1.call-update) | async-done | bytes 4915216 | tf_op jit(solution)/shard_map/all_gather | solution.py:107
  110.5 15.0 %bitcast_reduce_fusion = (f32[2,5,3,256]{3,2,1,0:T(4,128)S(1)}, f32[2,5,1024,256,3]{3,2,4,1,0:T(8,128)}) fusion(bf16[2,256,5,3,32]{1,4,3,2,0:T(8,128)(2,1)S(1)} %bitcast.322, bf16[2,256,5,3,32]{1,4,3,2,0:T(8,128)(2,1)} %bitcast.324, bf16[2,1024,5,64]{1,3,2,0:T(8,128)(2,1)} %all-gather.20.cloned.1.call-done, pred[2,1024]{1,0:T(4,128)(4,1)S(1)} %get-tuple-element.98), kind=kOutput, calls=%fused_computation.12 | convolution fusion | flops 1032184320 | bytes 33783808 | tf_op jit(solution)/shard_map/bqgrh,bkgh->bgrqk/dot_general | solution.py:54
  125.5 13.0 %fusion.11 = f32[2,5,3,256]{3,2,1,0:T(4,128)S(1)} fusion(f32[2,5,1024,256,3]{3,2,4,1,0:T(8,128)} %get-tuple-element.100, f32[2,5,3,256]{3,2,1,0:T(4,128)S(1)} %get-tuple-element.99), kind=kLoop, calls=%fused_computation.25 | loop fusion | flops 15720960 | bytes 31518720 | tf_op jit(solution)/shard_map/reduce_sum | solution.py:134
  138.5 14.3 %bitcast_reduce_fusion.1 = (f32[2,5,3,256]{3,2,1,0:T(4,128)S(1)}, f32[2,5,1024,256,3]{3,2,4,1,0:T(8,128)}) fusion(bf16[2,256,5,3,32]{1,4,3,2,0:T(8,128)(2,1)S(1)} %bitcast.320, bf16[2,256,5,3,32]{1,4,3,2,0:T(8,128)(2,1)S(1)} %bitcast.318, bf16[2,1024,5,64]{1,3,2,0:T(8,128)(2,1)} %all-gather.12.cloned.1.call-done, pred[2,1024]{1,0:T(4,128)(4,1)S(1)} %get-tuple-element.97), kind=kOutput, calls=%fused_computation.17 | convolution fusion | flops 1032184320 | bytes 33783808 | tf_op jit(solution)/shard_map/bqgrh,bkgh->bgrqk/dot_general | solution.py:54
  152.8 13.1 %fusion.10 = f32[2,5,3,256]{3,2,1,0:T(4,128)S(1)} fusion(f32[2,5,1024,256,3]{3,2,4,1,0:T(8,128)} %get-tuple-element.102, f32[2,5,3,256]{3,2,1,0:T(4,128)S(1)} %get-tuple-element.101), kind=kLoop, calls=%fused_computation.24 | loop fusion | flops 15720960 | bytes 31518720 | tf_op jit(solution)/shard_map/reduce_sum | solution.py:134
  166.0 13.3 %fusion.72 = bf16[2,5,64,3,256]{4,2,3,1,0:T(8,128)(2,1)S(1)} fusion(f32[2,5,1024,256,3]{3,2,4,1,0:T(8,128)} %get-tuple-element.100, f32[2,5,3,256]{3,2,1,0:T(4,128)S(1)} %fusion.11, f32[2,5,3,256]{3,2,1,0:T(4,128)S(1)} %get-tuple-element.99, bf16[2,1024,5,64]{1,3,2,0:T(8,128)(2,1)} %all-gather.18.cloned.1.call-done), kind=kOutput, calls=%fused_computation.144 | convolution fusion | flops 1030717440 | bytes 33812480 | tf_op jit(solution)/shard_map/bgrqk,bkgh->bqgrh/dot_general | solution.py:137
  183.7 13.5 %fusion.73 = bf16[2,5,64,3,256]{4,2,3,1,0:T(8,128)(2,1)S(1)} fusion(f32[2,5,1024,256,3]{3,2,4,1,0:T(8,128)} %get-tuple-element.102, f32[2,5,3,256]{3,2,1,0:T(4,128)S(1)} %fusion.10, f32[2,5,3,256]{3,2,1,0:T(4,128)S(1)} %get-tuple-element.101, bf16[2,1024,5,64]{1,3,2,0:T(8,128)(2,1)} %all-gather.10.cloned.1.call-done), kind=kOutput, calls=%fused_computation.145 | convolution fusion | flops 1030717440 | bytes 33812480 | tf_op jit(solution)/shard_map/bgrqk,bkgh->bqgrh/dot_general | solution.py:137
  203.7 50.6 %all-gather.14.cloned.1.call-done = bf16[960,5120]{0,1:T(8,128)(2,1)} async-done(((bf16[960,160]{0,1:T(8,128)(2,1)}), bf16[960,5120]{0,1:T(8,128)(2,1)}) %all-gather.14.cloned.1.call-update) | async-done | bytes 9830416 | tf_op jit(solution)/shard_map/all_gather | solution.py:108
  284.5 36.5 %all-gather.16.cloned.1.call-done = bf16[960,2560]{0,1:T(8,128)(2,1)} async-done(((bf16[960,80]{0,1:T(8,128)(2,1)}), bf16[960,2560]{0,1:T(8,128)(2,1)}) %all-gather.16.cloned.1.call-update) | async-done | bytes 4915216 | tf_op jit(solution)/shard_map/all_gather | solution.py:109
  361.1 13.9 %fusion.25 = f32[2,256,960]{1,2,0:T(8,128)} fusion(bf16[960,5120]{0,1:T(8,128)(2,1)} %all-gather.14.cloned.1.call-done, bf16[2,256,2560]{2,1,0:T(8,128)(2,1)} %get-tuple-element.37, bf16[2,256,2560]{2,1,0:T(8,128)(2,1)S(1)} %get-tuple-element.36), kind=kOutput, calls=%fused_computation.38 | convolution fusion | flops 5043650560 | bytes 17039360 | tf_op jit(solution)/shard_map/dot_general | solution.py:66
  375.0 15.0 %multiply_reduce_fusion = (f32[960]{0:T(1024)}, f32[2,256]{1,0:T(2,128)S(1)}, f32[2,256]{1,0:T(2,128)S(1)}, f32[960]{0:T(1024)}, f32[2,256,960]{1,2,0:T(8,128)}) fusion(f32[2,256,960]{1,2,0:T(8,128)} %get-tuple-element.53, f32[2,256]{1,0:T(2,128)S(1)} %get-tuple-element.90, f32[960]{0:T(1024)S(1)} %bitcast.340, f32[2,256,960]{1,2,0:T(8,128)} %get-tuple-element.31, ...), kind=kOutput, calls=%fused_computation.116 | convolution fusion | flops 5049545728 | bytes 22957312 | tf_op jit(solution)/shard_map/dot_general | solution.py:66
  399.2 24.1 %fusion = (f32[2,5,3,256]{3,2,1,0:T(4,128)S(1)}, f32[2,5,1024,256,3]{3,2,4,1,0:T(8,128)}) fusion(f32[2,5,1024,256,3]{3,2,4,1,0:T(8,128)} %get-tuple-element.100, f32[2,5,3,256]{3,2,1,0:T(4,128)S(1)} %log_add_fusion, bf16[2,256,5,3,64]{1,4,3,2,0:T(8,128)(2,1)S(1)} %bitcast.312, bf16[2,1024,5,64]{1,3,2,0:T(8,128)(2,1)S(1)} %copy-done.26), kind=kOutput, calls=%fused_computation.2 | convolution fusion | flops 1030218240 | bytes 65269760 | tf_op jit(solution)/shard_map/bqgrh,bkgh->bgrqk/dot_general | solution.py:187
  423.3 26.8 %fusion.2 = bf16[2,5,3,256,1024]{3,4,2,1,0:T(8,128)(2,1)} fusion(f32[2,5,1024,256,3]{3,2,4,1,0:T(8,128)} %get-tuple-element.106, f32[2,5,1024,256,3]{3,2,4,1,0:T(8,128)} %get-tuple-element.100, f32[2,5,3,256]{3,2,1,0:T(4,128)S(1)} %get-tuple-element.105, f32[2,5,3,256]{3,2,1,0:T(4,128)S(1)} %log_add_fusion), kind=kLoop, calls=%fused_computation.4 | loop fusion | flops 31457280 | bytes 78704640 | tf_op jit(solution)/shard_map/convert_element_type | solution.py:190
  464.7 24.4 %fusion.3 = (f32[2,5,3,256]{3,2,1,0:T(4,128)S(1)}, f32[2,5,1024,256,3]{3,2,4,1,0:T(8,128)}) fusion(f32[2,5,1024,256,3]{3,2,4,1,0:T(8,128)} %get-tuple-element.102, f32[2,5,3,256]{3,2,1,0:T(4,128)S(1)} %copy-done.30, bf16[2,256,5,3,64]{1,4,3,2,0:T(8,128)(2,1)S(1)} %bitcast.310, bf16[2,1024,5,64]{1,3,2,0:T(8,128)(2,1)S(1)} %copy-done.25), kind=kOutput, calls=%fused_computation.7 | convolution fusion | flops 1030218240 | bytes 65269760 | tf_op jit(solution)/shard_map/bqgrh,bkgh->bgrqk/dot_general | solution.py:187
  489.1 26.6 %fusion.5 = bf16[2,5,3,256,1024]{3,4,2,1,0:T(8,128)(2,1)} fusion(f32[2,5,1024,256,3]{3,2,4,1,0:T(8,128)} %get-tuple-element.108, f32[2,5,1024,256,3]{3,2,4,1,0:T(8,128)} %get-tuple-element.102, f32[2,5,3,256]{3,2,1,0:T(4,128)S(1)} %get-tuple-element.107, f32[2,5,3,256]{3,2,1,0:T(4,128)S(1)} %copy-done.30), kind=kLoop, calls=%fused_computation.9 | loop fusion | flops 31457280 | bytes 78704640 | tf_op jit(solution)/shard_map/convert_element_type | solution.py:190
  527.3 14.8 %fusion.77 = bf16[2,1024,5,64]{1,3,2,0:T(8,128)(2,1)} fusion(bf16[2,256,5,3,64]{1,4,3,2,0:T(8,128)(2,1)} %bitcast.313, f32[2,5,1024,256,3]{3,2,4,1,0:T(8,128)} %get-tuple-element.100, f32[2,5,3,256]{3,2,1,0:T(4,128)S(1)} %log_add_fusion), kind=kOutput, calls=%fused_computation.147 | convolution fusion | flops 1023016960 | bytes 33781760 | tf_op jit(solution)/shard_map/bgrqk,bqgrh->bkgh/dot_general | solution.py:203
  570.1 14.1 %fusion.74 = bf16[2,1024,5,64]{1,3,2,0:T(8,128)(2,1)} fusion(bf16[2,256,5,3,64]{1,4,3,2,0:T(8,128)(2,1)S(1)} %bitcast.311, f32[2,5,1024,256,3]{3,2,4,1,0:T(8,128)} %get-tuple-element.102, f32[2,5,3,256]{3,2,1,0:T(4,128)S(1)} %copy-done.30), kind=kOutput, calls=%fused_computation.146 | convolution fusion | flops 1023016960 | bytes 33781760 | tf_op jit(solution)/shard_map/bgrqk,bqgrh->bkgh/dot_general | solution.py:203
  608.3 35.2 %all-to-all-done.4 = bf16[960,8,4,80]{0,3,1,2:T(8,128)(2,1)} async-done(((bf16[960,8,4,80]{0,3,1,2:T(8,128)(2,1)}), bf16[960,8,4,80]{0,3,1,2:T(8,128)(2,1)}, u32[]{:S(2)}, u32[]{:S(2)}) %all-to-all-start.4) | async-done | bytes 4915232 | tf_op jit(solution)/shard_map/all_to_all | solution.py:253
  700.1 12.3 %fusion.41 = f32[960,5120,1]{1,0,2:T(8,128)} fusion(bf16[2,256,2560]{2,1,0:T(8,128)(2,1)} %get-tuple-element.37, bf16[2,256,2560]{2,1,0:T(8,128)(2,1)} %copy-done.95, f32[2,256,960]{1,2,0:T(8,128)} %get-tuple-element.31, f32[960]{0:T(1024)S(1)} %bitcast.342, f32[2,256]{1,0:T(2,128)S(1)} %copy-done.56), kind=kOutput, calls=%fused_computation.84 | convolution fusion | flops 5045125120 | bytes 26875648 | tf_op jit(solution)/shard_map/dot_general | solution.py:60
  712.4 13.8 %fusion.14 = bf16[960,5120]{1,0:T(8,128)(2,1)} fusion(f32[960,5120,1]{1,0,2:T(8,128)} %fusion.41, bf16[2,256,2560]{2,1,0:T(8,128)(2,1)} %get-tuple-element.35, bf16[2,256,2560]{2,1,0:T(8,128)(2,1)} %get-tuple-element.34, f32[2,256,960]{1,2,0:T(8,128)} %get-tuple-element.53, f32[2,256]{1,0:T(2,128)S(1)} %copy-done.60, f32[960]{0:T(1024)S(1)} %bitcast.343), kind=kOutput, calls=%fused_computation.29 | convolution fusion | flops 5054955520 | bytes 36706048 | tf_op jit(solution)/shard_map/dot_general | solution.py:60
  726.1 14.2 %copy.57 = bf16[960,5120]{0,1:T(8,128)(2,1)} copy(bf16[960,5120]{1,0:T(8,128)(2,1)} %fusion.14) | data formatting | bytes 19660800 | tf_op jit(solution)/shard_map/convert_element_type | solution.py:247
  770.6 110.4 %all-to-all-done.2 = bf16[960,8,4,160]{0,3,1,2:T(8,128)(2,1)} async-done(((bf16[960,8,4,160]{0,3,1,2:T(8,128)(2,1)}), bf16[960,8,4,160]{0,3,1,2:T(8,128)(2,1)}, u32[]{:S(2)}, u32[]{:S(2)}) %all-to-all-start.2) | async-done | bytes 9830432 | tf_op jit(solution)/shard_map/all_to_all | solution.py:246
  897.2 21.3 %all-to-all-done.1 = bf16[960,8,80]{0,2,1:T(8,128)(2,1)} async-done(((bf16[960,8,80]{0,2,1:T(8,128)(2,1)}), bf16[960,8,80]{0,2,1:T(8,128)(2,1)}, u32[]{:S(2)}, u32[]{:S(2)}) %all-to-all-start.1) | async-done | bytes 1228832 | tf_op jit(solution)/shard_map/all_to_all | solution.py:263
  938.1 63.9 %all-reduce = (f32[]{:T(128)}, f32[]{:T(128)}, f32[2,960]{1,0:T(2,128)}, f32[960]{0:T(1024)}) all-reduce(f32[]{:T(128)S(6)} %add.239, f32[]{:T(128)} %convert_reduce_fusion.3, f32[2,960]{1,0:T(2,128)S(1)} %pad_maximum_fusion.26, f32[960]{0:T(1024)S(1)} %add.263), channel_id=1, replica_groups=mesh['dp'=8,'ctx'=4] {'dp','ctx'}, use_global_device_ids=true, to_apply=%region_10.11 | all-reduce | flops 2882 | bytes 23056 | tf_op jit(solution)/shard_map/psum | solution.py:275
  (333 shorter events, 339.7 us)
Async XLA Ops:
  7.2 71.7 %all-gather.8.cloned.1.call-start = ((), (), s32[]{:S(2)}) async-start(), calls=%async_computation.10 | async-start | bytes 5406720 | tf_op jit(solution)/shard_map/all_gather | solution.py:107
  7.9 102.6 %all-gather.20.cloned.1.call-start = ((), (), s32[]{:S(2)}) async-start(), calls=%async_computation.16 | async-start | bytes 1638400 | tf_op jit(solution)/shard_map/all_gather | solution.py:126
  10.5 379.4 %copy-start.44 = (f32[1,960]{1,0:T(1,128)}, f32[1,960]{1,0:T(1,128)S(1)}, u32[]{:S(2)}) copy-start(f32[1,960]{1,0:T(1,128)S(1)} %get-tuple-element.70) | copy-start | bytes 11524
  10.7 96.1 %copy-start.38 = (f32[256,32]{0,1:T(8,128)}, f32[256,32]{0,1:T(8,128)S(1)}, u32[]{:S(2)}) copy-start(f32[256,32]{0,1:T(8,128)S(1)} %get-tuple-element.95) | copy-start | bytes 98308
  87.7 50.7 %all-gather.12.cloned.1.call-start = ((), (), s32[]{:S(2)}) async-start(), calls=%async_computation.12 | async-start | bytes 1638400 | tf_op jit(solution)/shard_map/all_gather | solution.py:126
  88.5 77.4 %all-gather.18.cloned.1.call-start = ((), (), s32[]{:S(2)}) async-start(), calls=%async_computation.15 | async-start | bytes 1638400 | tf_op jit(solution)/shard_map/all_gather | solution.py:127
  90.5 93.2 %all-gather.10.cloned.1.call-start = ((), (), s32[]{:S(2)}) async-start(), calls=%async_computation.11 | async-start | bytes 1638400 | tf_op jit(solution)/shard_map/all_gather | solution.py:127
  92.4 161.9 %all-gather.14.cloned.1.call-start = ((), (), s32[]{:S(2)}) async-start(), calls=%async_computation.13 | async-start | bytes 10813440 | tf_op jit(solution)/shard_map/all_gather | solution.py:108
  93.0 228.0 %all-gather.16.cloned.1.call-start = ((), (), s32[]{:S(2)}) async-start(), calls=%async_computation.14 | async-start | bytes 5406720 | tf_op jit(solution)/shard_map/all_gather | solution.py:109
  93.7 564.2 %reduce-scatter.9.cloned.1.call-start = ((), (), s32[]{:S(2)}) async-start(), calls=%async_computation.19 | async-start | bytes 1638400 | tf_op jit(solution)/shard_map/reduce_scatter | solution.py:210
  203.0 187.0 %copy-start.53 = (f32[2,256]{1,0:T(2,128)}, f32[2,256]{1,0:T(2,128)S(1)}, u32[]{:S(2)}) copy-start(f32[2,256]{1,0:T(2,128)S(1)} %get-tuple-element.91) | copy-start | bytes 6148
  203.0 187.0 %copy-start.55 = (f32[2,256]{1,0:T(2,128)}, f32[2,256]{1,0:T(2,128)S(1)}, u32[]{:S(2)}) copy-start(f32[2,256]{1,0:T(2,128)S(1)} %get-tuple-element.92) | copy-start | bytes 6148
  203.0 187.0 %copy-start.57 = (f32[2,256]{1,0:T(2,128)}, f32[2,256]{1,0:T(2,128)S(1)}, u32[]{:S(2)}) copy-start(f32[2,256]{1,0:T(2,128)S(1)} %get-tuple-element.89) | copy-start | bytes 6148
  203.0 187.0 %copy-start.59 = (f32[2,256]{1,0:T(2,128)}, f32[2,256]{1,0:T(2,128)S(1)}, u32[]{:S(2)}) copy-start(f32[2,256]{1,0:T(2,128)S(1)} %get-tuple-element.90) | copy-start | bytes 6148
  461.5 198.3 %reduce-scatter.5.cloned.1.call-start = ((), (), s32[]{:S(2)}) async-start(), calls=%async_computation.17 | async-start | bytes 1638400 | tf_op jit(solution)/shard_map/reduce_scatter | solution.py:210
  527.3 136.5 %reduce-scatter.11.cloned.1.call-start = ((), (), s32[]{:S(2)}) async-start(), calls=%async_computation.20 | async-start | bytes 1638400 | tf_op jit(solution)/shard_map/reduce_scatter | solution.py:213
  564.9 78.5 %all-to-all-start.4 = ((bf16[960,8,4,80]{0,3,1,2:T(8,128)(2,1)}), bf16[960,8,4,80]{0,3,1,2:T(8,128)(2,1)}, u32[]{:S(2)}, u32[]{:S(2)}) async-start(bf16[960,8,4,80]{0,3,1,2:T(8,128)(2,1)} %copy.61), calls=%async_computation.8 | async-start | bytes 10485760 | tf_op jit(solution)/shard_map/all_to_all | solution.py:253
  570.0 99.9 %reduce-scatter.7.cloned.1.call-start = ((), (), s32[]{:S(2)}) async-start(), calls=%async_computation.18 | async-start | bytes 1638400 | tf_op jit(solution)/shard_map/reduce_scatter | solution.py:213
  648.7 46.1 %all-to-all-start.5 = ((bf16[960,8,80]{0,2,1:T(8,128)(2,1)}), bf16[960,8,80]{0,2,1:T(8,128)(2,1)S(1)}, u32[]{:S(2)}, u32[]{:S(2)}) async-start(bf16[960,8,80]{0,2,1:T(8,128)(2,1)} %reduce_sum.273), calls=%async_computation.9 | async-start | bytes 2621440 | tf_op jit(solution)/shard_map/all_to_all | solution.py:269
  694.8 64.7 %all-to-all-start = ((bf16[960,8,4,80]{0,3,1,2:T(8,128)(2,1)}), bf16[960,8,4,80]{0,3,1,2:T(8,128)(2,1)}, u32[]{:S(2)}, u32[]{:S(2)}) async-start(bf16[960,8,4,80]{0,3,1,2:T(8,128)(2,1)} %copy.55), calls=%async_computation.4 | async-start | bytes 10485760 | tf_op jit(solution)/shard_map/all_to_all | solution.py:239
  759.5 121.6 %all-to-all-start.2 = ((bf16[960,8,4,160]{0,3,1,2:T(8,128)(2,1)}), bf16[960,8,4,160]{0,3,1,2:T(8,128)(2,1)}, u32[]{:S(2)}, u32[]{:S(2)}) async-start(bf16[960,8,4,160]{0,3,1,2:T(8,128)(2,1)} %copy.58), calls=%async_computation.6 | async-start | bytes 20971520 | tf_op jit(solution)/shard_map/all_to_all | solution.py:246
  770.6 116.7 %copy-start.70 = (s32[4,256]{1,0:T(4,128)S(1)}, s32[4,256]{1,0:T(4,128)}, u32[]{:S(2)}) copy-start(s32[4,256]{1,0:T(4,128)} %param.11) | copy-start | bytes 12292
  881.0 37.4 %all-to-all-start.1 = ((bf16[960,8,80]{0,2,1:T(8,128)(2,1)}), bf16[960,8,80]{0,2,1:T(8,128)(2,1)}, u32[]{:S(2)}, u32[]{:S(2)}) async-start(bf16[960,8,80]{0,2,1:T(8,128)(2,1)} %reduce_sum.269), calls=%async_computation.5 | async-start | bytes 2621440 | tf_op jit(solution)/shard_map/all_to_all | solution.py:263
  918.4 97.5 %all-to-all-start.3 = ((bf16[960,8,160]{0,2,1:T(8,128)(2,1)}), bf16[960,8,160]{0,2,1:T(8,128)(2,1)}, u32[]{:S(2)}, u32[]{:S(2)}) async-start(bf16[960,8,160]{0,2,1:T(8,128)(2,1)} %reduce_sum.271), calls=%async_computation.7 | async-start | bytes 5242880 | tf_op jit(solution)/shard_map/all_to_all | solution.py:266
  (94 other events, 1399.9 us)
Sparse Core Ops, SparseCore 0:
  10.8 68.0 all-gather.7
  87.8 16.8 all-gather.19
  106.9 18.3 all-gather.11
  127.2 18.3 all-gather.17
  146.9 18.3 all-gather.9
  168.0 86.2 all-gather.13
  257.1 63.8 all-gather.15
  461.7 24.9 reduce-scatter.8
  527.4 24.9 reduce-scatter.4
  555.3 33.5 reduce-scatter.10
  591.5 33.5 reduce-scatter.6
where the time goes:
time: 1030 us
  matrix products  347 us (34%)
  waiting for transfers between devices  333 us (32%)
  other arithmetic  149 us (14%)
  blocking collectives  74.7 us (7%)
  local copies, waits for them, and re-layouts  71.1 us (7%)
  starting transfers between devices  31.9 us (3%)
  between operations  19.2 us (2%)
    all_to_all x1, waiting for transfers between devices, on_device(): lax.all_to_all(owner_layout(grad_gu).astype(jnp.bfloat16), 'ctx', split_a...  110 us
    all_gather x1, waiting for transfers between devices, on_device(): lax.all_gather(packs[0], ('dp', 'ctx'), axis=1, tiled=True)  68.1 us
    dot_general x8, matrix products, by_columns(): lax.dot_general(left, right, (((2,), (1,)), ((), ())), preferred_element_...  67.6 us
    psum x1, blocking collectives, on_device(): lax.psum((energy, grad_gains, grad_router), ('dp', 'ctx'))  63.9 us
    convert_element_type x2, other arithmetic, on_device(): (probs * (d_probs - jnp.sum(probs * d_probs, axis=-1, keepdims=True))).as...  53.3 us
    dot_general x8, matrix products, over_rows(): lax.dot_general(left, right, (((0, 1), (0, 1)), ((), ())), preferred_elem...  51 us
    all_gather x1, waiting for transfers between devices, on_device(): lax.all_gather(packs[1], ('dp', 'ctx'), axis=1, tiled=True)  50.6 us
    dot_general x2, matrix products, on_device(): jnp.einsum('bqgrh,bkgh->bgrqk', d_heads_low, values_all, preferred_elemen...  48.6 us
  transfers between devices with their start and end apart: 17, of which 7 were waited for; matrix products, arithmetic and copies ran while one was open for 39% of the time, Pallas kernels for 0%

commit v1 on v0

--- a/solution.py
+++ b/solution.py
@@ -260,9 +260,12 @@
     )
     attn_ctx, gu_ctx, down_ctx = [jnp.sum(piece, axis=2) for piece in by_ctx]
     by_dp = (
-        lax.all_to_all(shortened(attn_ctx), "dp", split_axis=1, concat_axis=1, tiled=True).astype(
-            attn_ctx.dtype
-        ),
+        jnp.concatenate(
+            lax.all_to_all(
+                jnp.stack(jnp.split(shortened(attn_ctx), lax.axis_size("dp"), axis=1)), "dp", 0, 0
+            ),
+            axis=1,
+        ).astype(attn_ctx.dtype),
         lax.all_to_all(shortened(gu_ctx), "dp", split_axis=1, concat_axis=1, tiled=True).astype(
             gu_ctx.dtype
         ),

time: 1030 us -> 1030 us (level)
  local copies, waits for them, and re-layouts: 71.1 us -> 83.9 us
  waiting for transfers between devices: 333 us -> 321 us
    all_to_all x1, waiting for transfers between devices: 110 us -> 97.7 us  [on_device(): lax.all_to_all(owner_layout(grad_gu).astype(jnp.bfloat16), 'ctx', split_a...]
    unnamed x198 -> x205, local copies, waits for them, and re-layouts: 13.2 us -> 24.4 us
  transfers between devices with their start and end apart: 17 -> 17, of which waited for: 7 -> 7; matrix products, arithmetic and copies ran while one was open for 39% -> 40% of each run, Pallas kernels for 0% -> 0%
where the time goes in v1:
time: 1030 us
  matrix products  347 us (34%)
  waiting for transfers between devices  321 us (31%)
  other arithmetic  149 us (14%)
  local copies, waits for them, and re-layouts  83.9 us (8%)
  blocking collectives  74.7 us (7%)
  starting transfers between devices  31.9 us (3%)
  between operations  19.2 us (2%)
    all_to_all x1, waiting for transfers between devices, on_device(): lax.all_to_all(owner_layout(grad_gu).astype(jnp.bfloat16), 'ctx', split_a...  97.7 us
    all_gather x1, waiting for transfers between devices, on_device(): lax.all_gather(packs[0], ('dp', 'ctx'), axis=1, tiled=True)  68.1 us
    dot_general x8, matrix products, by_columns(): lax.dot_general(left, right, (((2,), (1,)), ((), ())), preferred_element_...  67.6 us
    psum x1, blocking collectives, on_device(): lax.psum((energy, grad_gains, grad_router), ('dp', 'ctx'))  63.9 us
    convert_element_type x2, other arithmetic, on_device(): (probs * (d_probs - jnp.sum(probs * d_probs, axis=-1, keepdims=True))).as...  53.3 us
    dot_general x8, matrix products, over_rows(): lax.dot_general(left, right, (((0, 1), (0, 1)), ((), ())), preferred_elem...  51 us
    all_gather x1, waiting for transfers between devices, on_device(): lax.all_gather(packs[1], ('dp', 'ctx'), axis=1, tiled=True)  50.6 us
    dot_general x2, matrix products, on_device(): jnp.einsum('bqgrh,bkgh->bgrqk', d_heads_low, values_all, preferred_elemen...  48.6 us
  transfers between devices with their start and end apart: 17, of which 7 were waited for; matrix products, arithmetic and copies ran while one was open for 40% of the time, Pallas kernels for 0%

profile of v1, /device:TPU:0, one launch (start us, length us, event | category | flops | bytes accessed | tf_op | source)
XLA Modules:
  0.0 1026.9 jit_solution(2927333009687302043)
XLA Ops:
  10.8 68.1 %all-gather.8.cloned.1.call-done = bf16[960,2560]{0,1:T(8,128)(2,1)} async-done(((bf16[960,80]{0,1:T(8,128)(2,1)}), bf16[960,2560]{0,1:T(8,128)(2,1)}) %all-gather.8.cloned.1.call-update) | async-done | bytes 4915216 | tf_op jit(solution)/shard_map/all_gather | solution.py:107
  110.5 15.0 %bitcast_reduce_fusion = (f32[2,5,3,256]{3,2,1,0:T(4,128)S(1)}, f32[2,5,1024,256,3]{3,2,4,1,0:T(8,128)}) fusion(bf16[2,256,5,3,32]{1,4,3,2,0:T(8,128)(2,1)S(1)} %bitcast.354, bf16[2,256,5,3,32]{1,4,3,2,0:T(8,128)(2,1)} %bitcast.356, bf16[2,1024,5,64]{1,3,2,0:T(8,128)(2,1)} %all-gather.20.cloned.1.call-done, pred[2,1024]{1,0:T(4,128)(4,1)S(1)} %get-tuple-element.98), kind=kOutput, calls=%fused_computation.12 | convolution fusion | flops 1032184320 | bytes 33783808 | tf_op jit(solution)/shard_map/bqgrh,bkgh->bgrqk/dot_general | solution.py:54
  125.5 13.0 %fusion.11 = f32[2,5,3,256]{3,2,1,0:T(4,128)S(1)} fusion(f32[2,5,1024,256,3]{3,2,4,1,0:T(8,128)} %get-tuple-element.100, f32[2,5,3,256]{3,2,1,0:T(4,128)S(1)} %get-tuple-element.99), kind=kLoop, calls=%fused_computation.25 | loop fusion | flops 15720960 | bytes 31518720 | tf_op jit(solution)/shard_map/reduce_sum | solution.py:134
  138.5 14.3 %bitcast_reduce_fusion.1 = (f32[2,5,3,256]{3,2,1,0:T(4,128)S(1)}, f32[2,5,1024,256,3]{3,2,4,1,0:T(8,128)}) fusion(bf16[2,256,5,3,32]{1,4,3,2,0:T(8,128)(2,1)S(1)} %bitcast.352, bf16[2,256,5,3,32]{1,4,3,2,0:T(8,128)(2,1)S(1)} %bitcast.350, bf16[2,1024,5,64]{1,3,2,0:T(8,128)(2,1)} %all-gather.12.cloned.1.call-done, pred[2,1024]{1,0:T(4,128)(4,1)S(1)} %get-tuple-element.97), kind=kOutput, calls=%fused_computation.17 | convolution fusion | flops 1032184320 | bytes 33783808 | tf_op jit(solution)/shard_map/bqgrh,bkgh->bgrqk/dot_general | solution.py:54
  152.8 13.1 %fusion.10 = f32[2,5,3,256]{3,2,1,0:T(4,128)S(1)} fusion(f32[2,5,1024,256,3]{3,2,4,1,0:T(8,128)} %get-tuple-element.102, f32[2,5,3,256]{3,2,1,0:T(4,128)S(1)} %get-tuple-element.101), kind=kLoop, calls=%fused_computation.24 | loop fusion | flops 15720960 | bytes 31518720 | tf_op jit(solution)/shard_map/reduce_sum | solution.py:134
  166.0 13.3 %fusion.72 = bf16[2,5,64,3,256]{4,2,3,1,0:T(8,128)(2,1)S(1)} fusion(f32[2,5,1024,256,3]{3,2,4,1,0:T(8,128)} %get-tuple-element.100, f32[2,5,3,256]{3,2,1,0:T(4,128)S(1)} %fusion.11, f32[2,5,3,256]{3,2,1,0:T(4,128)S(1)} %get-tuple-element.99, bf16[2,1024,5,64]{1,3,2,0:T(8,128)(2,1)} %all-gather.18.cloned.1.call-done), kind=kOutput, calls=%fused_computation.144 | convolution fusion | flops 1030717440 | bytes 33812480 | tf_op jit(solution)/shard_map/bgrqk,bkgh->bqgrh/dot_general | solution.py:137
  183.7 13.5 %fusion.73 = bf16[2,5,64,3,256]{4,2,3,1,0:T(8,128)(2,1)S(1)} fusion(f32[2,5,1024,256,3]{3,2,4,1,0:T(8,128)} %get-tuple-element.102, f32[2,5,3,256]{3,2,1,0:T(4,128)S(1)} %fusion.10, f32[2,5,3,256]{3,2,1,0:T(4,128)S(1)} %get-tuple-element.101, bf16[2,1024,5,64]{1,3,2,0:T(8,128)(2,1)} %all-gather.10.cloned.1.call-done), kind=kOutput, calls=%fused_computation.145 | convolution fusion | flops 1030717440 | bytes 33812480 | tf_op jit(solution)/shard_map/bgrqk,bkgh->bqgrh/dot_general | solution.py:137
  203.7 50.6 %all-gather.14.cloned.1.call-done = bf16[960,5120]{0,1:T(8,128)(2,1)} async-done(((bf16[960,160]{0,1:T(8,128)(2,1)}), bf16[960,5120]{0,1:T(8,128)(2,1)}) %all-gather.14.cloned.1.call-update) | async-done | bytes 9830416 | tf_op jit(solution)/shard_map/all_gather | solution.py:108
  284.5 36.5 %all-gather.16.cloned.1.call-done = bf16[960,2560]{0,1:T(8,128)(2,1)} async-done(((bf16[960,80]{0,1:T(8,128)(2,1)}), bf16[960,2560]{0,1:T(8,128)(2,1)}) %all-gather.16.cloned.1.call-update) | async-done | bytes 4915216 | tf_op jit(solution)/shard_map/all_gather | solution.py:109
  361.1 13.9 %fusion.25 = f32[2,256,960]{1,2,0:T(8,128)} fusion(bf16[960,5120]{0,1:T(8,128)(2,1)} %all-gather.14.cloned.1.call-done, bf16[2,256,2560]{2,1,0:T(8,128)(2,1)} %get-tuple-element.37, bf16[2,256,2560]{2,1,0:T(8,128)(2,1)S(1)} %get-tuple-element.36), kind=kOutput, calls=%fused_computation.38 | convolution fusion | flops 5043650560 | bytes 17039360 | tf_op jit(solution)/shard_map/dot_general | solution.py:66
  375.0 15.0 %multiply_reduce_fusion = (f32[960]{0:T(1024)}, f32[2,256]{1,0:T(2,128)S(1)}, f32[2,256]{1,0:T(2,128)S(1)}, f32[960]{0:T(1024)}, f32[2,256,960]{1,2,0:T(8,128)}) fusion(f32[2,256,960]{1,2,0:T(8,128)} %get-tuple-element.53, f32[2,256]{1,0:T(2,128)S(1)} %get-tuple-element.90, f32[960]{0:T(1024)S(1)} %bitcast.372, f32[2,256,960]{1,2,0:T(8,128)} %get-tuple-element.31, ...), kind=kOutput, calls=%fused_computation.116 | convolution fusion | flops 5049545728 | bytes 22957312 | tf_op jit(solution)/shard_map/dot_general | solution.py:66
  399.2 24.1 %fusion = (f32[2,5,3,256]{3,2,1,0:T(4,128)S(1)}, f32[2,5,1024,256,3]{3,2,4,1,0:T(8,128)}) fusion(f32[2,5,1024,256,3]{3,2,4,1,0:T(8,128)} %get-tuple-element.100, f32[2,5,3,256]{3,2,1,0:T(4,128)S(1)} %log_add_fusion, bf16[2,256,5,3,64]{1,4,3,2,0:T(8,128)(2,1)S(1)} %bitcast.344, bf16[2,1024,5,64]{1,3,2,0:T(8,128)(2,1)S(1)} %copy-done.26), kind=kOutput, calls=%fused_computation.2 | convolution fusion | flops 1030218240 | bytes 65269760 | tf_op jit(solution)/shard_map/bqgrh,bkgh->bgrqk/dot_general | solution.py:187
  423.3 26.8 %fusion.2 = bf16[2,5,3,256,1024]{3,4,2,1,0:T(8,128)(2,1)} fusion(f32[2,5,1024,256,3]{3,2,4,1,0:T(8,128)} %get-tuple-element.106, f32[2,5,1024,256,3]{3,2,4,1,0:T(8,128)} %get-tuple-element.100, f32[2,5,3,256]{3,2,1,0:T(4,128)S(1)} %get-tuple-element.105, f32[2,5,3,256]{3,2,1,0:T(4,128)S(1)} %log_add_fusion), kind=kLoop, calls=%fused_computation.4 | loop fusion | flops 31457280 | bytes 78704640 | tf_op jit(solution)/shard_map/convert_element_type | solution.py:190
  464.7 24.4 %fusion.3 = (f32[2,5,3,256]{3,2,1,0:T(4,128)S(1)}, f32[2,5,1024,256,3]{3,2,4,1,0:T(8,128)}) fusion(f32[2,5,1024,256,3]{3,2,4,1,0:T(8,128)} %get-tuple-element.102, f32[2,5,3,256]{3,2,1,0:T(4,128)S(1)} %copy-done.30, bf16[2,256,5,3,64]{1,4,3,2,0:T(8,128)(2,1)S(1)} %bitcast.342, bf16[2,1024,5,64]{1,3,2,0:T(8,128)(2,1)S(1)} %copy-done.25), kind=kOutput, calls=%fused_computation.7 | convolution fusion | flops 1030218240 | bytes 65269760 | tf_op jit(solution)/shard_map/bqgrh,bkgh->bgrqk/dot_general | solution.py:187
  489.1 26.6 %fusion.5 = bf16[2,5,3,256,1024]{3,4,2,1,0:T(8,128)(2,1)} fusion(f32[2,5,1024,256,3]{3,2,4,1,0:T(8,128)} %get-tuple-element.108, f32[2,5,1024,256,3]{3,2,4,1,0:T(8,128)} %get-tuple-element.102, f32[2,5,3,256]{3,2,1,0:T(4,128)S(1)} %get-tuple-element.107, f32[2,5,3,256]{3,2,1,0:T(4,128)S(1)} %copy-done.30), kind=kLoop, calls=%fused_computation.9 | loop fusion | flops 31457280 | bytes 78704640 | tf_op jit(solution)/shard_map/convert_element_type | solution.py:190
  527.3 14.8 %fusion.77 = bf16[2,1024,5,64]{1,3,2,0:T(8,128)(2,1)} fusion(bf16[2,256,5,3,64]{1,4,3,2,0:T(8,128)(2,1)} %bitcast.345, f32[2,5,1024,256,3]{3,2,4,1,0:T(8,128)} %get-tuple-element.100, f32[2,5,3,256]{3,2,1,0:T(4,128)S(1)} %log_add_fusion), kind=kOutput, calls=%fused_computation.147 | convolution fusion | flops 1023016960 | bytes 33781760 | tf_op jit(solution)/shard_map/bgrqk,bqgrh->bkgh/dot_general | solution.py:203
  570.1 14.1 %fusion.74 = bf16[2,1024,5,64]{1,3,2,0:T(8,128)(2,1)} fusion(bf16[2,256,5,3,64]{1,4,3,2,0:T(8,128)(2,1)S(1)} %bitcast.343, f32[2,5,1024,256,3]{3,2,4,1,0:T(8,128)} %get-tuple-element.102, f32[2,5,3,256]{3,2,1,0:T(4,128)S(1)} %copy-done.30), kind=kOutput, calls=%fused_computation.146 | convolution fusion | flops 1023016960 | bytes 33781760 | tf_op jit(solution)/shard_map/bgrqk,bqgrh->bkgh/dot_general | solution.py:203
  608.3 35.2 %all-to-all-done.4 = bf16[960,8,4,80]{0,3,1,2:T(8,128)(2,1)} async-done(((bf16[960,8,4,80]{0,3,1,2:T(8,128)(2,1)}), bf16[960,8,4,80]{0,3,1,2:T(8,128)(2,1)}, u32[]{:S(2)}, u32[]{:S(2)}) %all-to-all-start.4) | async-done | bytes 4915232 | tf_op jit(solution)/shard_map/all_to_all | solution.py:253
  700.1 12.3 %fusion.41 = f32[960,5120,1]{1,0,2:T(8,128)} fusion(bf16[2,256,2560]{2,1,0:T(8,128)(2,1)} %get-tuple-element.37, bf16[2,256,2560]{2,1,0:T(8,128)(2,1)} %copy-done.95, f32[2,256,960]{1,2,0:T(8,128)} %get-tuple-element.31, f32[960]{0:T(1024)S(1)} %bitcast.374, f32[2,256]{1,0:T(2,128)S(1)} %copy-done.56), kind=kOutput, calls=%fused_computation.84 | convolution fusion | flops 5045125120 | bytes 26875648 | tf_op jit(solution)/shard_map/dot_general | solution.py:60
  712.4 13.8 %fusion.14 = bf16[960,5120]{1,0:T(8,128)(2,1)} fusion(f32[960,5120,1]{1,0,2:T(8,128)} %fusion.41, bf16[2,256,2560]{2,1,0:T(8,128)(2,1)} %get-tuple-element.35, bf16[2,256,2560]{2,1,0:T(8,128)(2,1)} %get-tuple-element.34, f32[2,256,960]{1,2,0:T(8,128)} %get-tuple-element.53, f32[2,256]{1,0:T(2,128)S(1)} %copy-done.60, f32[960]{0:T(1024)S(1)} %bitcast.375), kind=kOutput, calls=%fused_computation.29 | convolution fusion | flops 5054955520 | bytes 36706048 | tf_op jit(solution)/shard_map/dot_general | solution.py:60
  726.1 14.2 %copy.63 = bf16[960,5120]{0,1:T(8,128)(2,1)} copy(bf16[960,5120]{1,0:T(8,128)(2,1)} %fusion.14) | data formatting | bytes 19660800 | tf_op jit(solution)/shard_map/convert_element_type | solution.py:247
  783.4 97.7 %all-to-all-done.2 = bf16[960,8,4,160]{0,3,1,2:T(8,128)(2,1)} async-done(((bf16[960,8,4,160]{0,3,1,2:T(8,128)(2,1)}), bf16[960,8,4,160]{0,3,1,2:T(8,128)(2,1)}, u32[]{:S(2)}, u32[]{:S(2)}) %all-to-all-start.2) | async-done | bytes 9830432 | tf_op jit(solution)/shard_map/all_to_all | solution.py:246
  897.2 21.3 %all-to-all-done.1 = bf16[8,960,1,80]{1,3,2,0:T(8,128)(2,1)} async-done(((bf16[8,960,1,80]{1,3,2,0:T(8,128)(2,1)}), bf16[8,960,1,80]{1,3,2,0:T(8,128)(2,1)}, u32[]{:S(2)}, u32[]{:S(2)}) %all-to-all-start.1) | async-done | bytes 1228832 | tf_op jit(solution)/shard_map/all_to_all | solution.py:264
  938.1 63.9 %all-reduce = (f32[]{:T(128)}, f32[]{:T(128)}, f32[2,960]{1,0:T(2,128)}, f32[960]{0:T(1024)}) all-reduce(f32[]{:T(128)S(6)} %add.239, f32[]{:T(128)} %convert_reduce_fusion.3, f32[2,960]{1,0:T(2,128)S(1)} %pad_maximum_fusion.26, f32[960]{0:T(1024)S(1)} %add.263), channel_id=1, replica_groups=mesh['dp'=8,'ctx'=4] {'dp','ctx'}, use_global_device_ids=true, to_apply=%region_10.11 | all-reduce | flops 2882 | bytes 23056 | tf_op jit(solution)/shard_map/psum | solution.py:278
  (341 shorter events, 352.4 us)
Async XLA Ops:
  7.2 71.7 %all-gather.8.cloned.1.call-start = ((), (), s32[]{:S(2)}) async-start(), calls=%async_computation.10 | async-start | bytes 5406720 | tf_op jit(solution)/shard_map/all_gather | solution.py:107
  7.9 102.6 %all-gather.20.cloned.1.call-start = ((), (), s32[]{:S(2)}) async-start(), calls=%async_computation.16 | async-start | bytes 1638400 | tf_op jit(solution)/shard_map/all_gather | solution.py:126
  10.5 379.4 %copy-start.44 = (f32[1,960]{1,0:T(1,128)}, f32[1,960]{1,0:T(1,128)S(1)}, u32[]{:S(2)}) copy-start(f32[1,960]{1,0:T(1,128)S(1)} %get-tuple-element.70) | copy-start | bytes 11524
  10.7 96.1 %copy-start.38 = (f32[256,32]{0,1:T(8,128)}, f32[256,32]{0,1:T(8,128)S(1)}, u32[]{:S(2)}) copy-start(f32[256,32]{0,1:T(8,128)S(1)} %get-tuple-element.95) | copy-start | bytes 98308
  87.7 50.7 %all-gather.12.cloned.1.call-start = ((), (), s32[]{:S(2)}) async-start(), calls=%async_computation.12 | async-start | bytes 1638400 | tf_op jit(solution)/shard_map/all_gather | solution.py:126
  88.5 77.4 %all-gather.18.cloned.1.call-start = ((), (), s32[]{:S(2)}) async-start(), calls=%async_computation.15 | async-start | bytes 1638400 | tf_op jit(solution)/shard_map/all_gather | solution.py:127
  90.5 93.2 %all-gather.10.cloned.1.call-start = ((), (), s32[]{:S(2)}) async-start(), calls=%async_computation.11 | async-start | bytes 1638400 | tf_op jit(solution)/shard_map/all_gather | solution.py:127
  92.4 161.9 %all-gather.14.cloned.1.call-start = ((), (), s32[]{:S(2)}) async-start(), calls=%async_computation.13 | async-start | bytes 10813440 | tf_op jit(solution)/shard_map/all_gather | solution.py:108
  93.0 228.0 %all-gather.16.cloned.1.call-start = ((), (), s32[]{:S(2)}) async-start(), calls=%async_computation.14 | async-start | bytes 5406720 | tf_op jit(solution)/shard_map/all_gather | solution.py:109
  93.7 564.2 %reduce-scatter.9.cloned.1.call-start = ((), (), s32[]{:S(2)}) async-start(), calls=%async_computation.19 | async-start | bytes 1638400 | tf_op jit(solution)/shard_map/reduce_scatter | solution.py:210
  203.0 187.0 %copy-start.53 = (f32[2,256]{1,0:T(2,128)}, f32[2,256]{1,0:T(2,128)S(1)}, u32[]{:S(2)}) copy-start(f32[2,256]{1,0:T(2,128)S(1)} %get-tuple-element.91) | copy-start | bytes 6148
  203.0 187.0 %copy-start.55 = (f32[2,256]{1,0:T(2,128)}, f32[2,256]{1,0:T(2,128)S(1)}, u32[]{:S(2)}) copy-start(f32[2,256]{1,0:T(2,128)S(1)} %get-tuple-element.92) | copy-start | bytes 6148
  203.0 187.0 %copy-start.57 = (f32[2,256]{1,0:T(2,128)}, f32[2,256]{1,0:T(2,128)S(1)}, u32[]{:S(2)}) copy-start(f32[2,256]{1,0:T(2,128)S(1)} %get-tuple-element.89) | copy-start | bytes 6148
  203.0 187.0 %copy-start.59 = (f32[2,256]{1,0:T(2,128)}, f32[2,256]{1,0:T(2,128)S(1)}, u32[]{:S(2)}) copy-start(f32[2,256]{1,0:T(2,128)S(1)} %get-tuple-element.90) | copy-start | bytes 6148
  461.5 198.3 %reduce-scatter.5.cloned.1.call-start = ((), (), s32[]{:S(2)}) async-start(), calls=%async_computation.17 | async-start | bytes 1638400 | tf_op jit(solution)/shard_map/reduce_scatter | solution.py:210
  527.3 136.5 %reduce-scatter.11.cloned.1.call-start = ((), (), s32[]{:S(2)}) async-start(), calls=%async_computation.20 | async-start | bytes 1638400 | tf_op jit(solution)/shard_map/reduce_scatter | solution.py:213
  564.9 78.5 %all-to-all-start.4 = ((bf16[960,8,4,80]{0,3,1,2:T(8,128)(2,1)}), bf16[960,8,4,80]{0,3,1,2:T(8,128)(2,1)}, u32[]{:S(2)}, u32[]{:S(2)}) async-start(bf16[960,8,4,80]{0,3,1,2:T(8,128)(2,1)} %copy.67), calls=%async_computation.8 | async-start | bytes 10485760 | tf_op jit(solution)/shard_map/all_to_all | solution.py:253
  570.0 99.9 %reduce-scatter.7.cloned.1.call-start = ((), (), s32[]{:S(2)}) async-start(), calls=%async_computation.18 | async-start | bytes 1638400 | tf_op jit(solution)/shard_map/reduce_scatter | solution.py:213
  648.7 46.1 %all-to-all-start.5 = ((bf16[960,8,80]{0,2,1:T(8,128)(2,1)}), bf16[960,8,80]{0,2,1:T(8,128)(2,1)S(1)}, u32[]{:S(2)}, u32[]{:S(2)}) async-start(bf16[960,8,80]{0,2,1:T(8,128)(2,1)} %reduce_sum.273), calls=%async_computation.9 | async-start | bytes 2621440 | tf_op jit(solution)/shard_map/all_to_all | solution.py:272
  694.8 64.7 %all-to-all-start = ((bf16[960,8,4,80]{0,3,1,2:T(8,128)(2,1)}), bf16[960,8,4,80]{0,3,1,2:T(8,128)(2,1)}, u32[]{:S(2)}, u32[]{:S(2)}) async-start(bf16[960,8,4,80]{0,3,1,2:T(8,128)(2,1)} %copy.62), calls=%async_computation.4 | async-start | bytes 10485760 | tf_op jit(solution)/shard_map/all_to_all | solution.py:239
  759.5 121.6 %all-to-all-start.2 = ((bf16[960,8,4,160]{0,3,1,2:T(8,128)(2,1)}), bf16[960,8,4,160]{0,3,1,2:T(8,128)(2,1)}, u32[]{:S(2)}, u32[]{:S(2)}) async-start(bf16[960,8,4,160]{0,3,1,2:T(8,128)(2,1)} %copy.64), calls=%async_computation.6 | async-start | bytes 20971520 | tf_op jit(solution)/shard_map/all_to_all | solution.py:246
  777.0 110.3 %copy-start.70 = (s32[4,256]{1,0:T(4,128)S(1)}, s32[4,256]{1,0:T(4,128)}, u32[]{:S(2)}) copy-start(s32[4,256]{1,0:T(4,128)} %param.11) | copy-start | bytes 12292
  881.0 37.4 %all-to-all-start.1 = ((bf16[8,960,1,80]{1,3,2,0:T(8,128)(2,1)}), bf16[8,960,1,80]{1,3,2,0:T(8,128)(2,1)}, u32[]{:S(2)}, u32[]{:S(2)}) async-start(bf16[8,960,1,80]{1,3,2,0:T(8,128)(2,1)} %fusion.105), calls=%async_computation.5 | async-start | bytes 2621440 | tf_op jit(solution)/shard_map/all_to_all | solution.py:264
  918.4 97.5 %all-to-all-start.3 = ((bf16[960,8,160]{0,2,1:T(8,128)(2,1)}), bf16[960,8,160]{0,2,1:T(8,128)(2,1)}, u32[]{:S(2)}, u32[]{:S(2)}) async-start(bf16[960,8,160]{0,2,1:T(8,128)(2,1)} %reduce_sum.271), calls=%async_computation.7 | async-start | bytes 5242880 | tf_op jit(solution)/shard_map/all_to_all | solution.py:269
  (94 other events, 1399.9 us)
Sparse Core Ops, SparseCore 0:
  10.8 68.0 all-gather.7
  87.8 16.8 all-gather.19
  106.9 18.3 all-gather.11
  127.2 18.3 all-gather.17
  146.9 18.3 all-gather.9
  168.0 86.2 all-gather.13
  257.1 63.8 all-gather.15
  461.7 24.9 reduce-scatter.8
  527.4 24.9 reduce-scatter.4
  555.3 33.5 reduce-scatter.10
  591.5 33.5 reduce-scatter.6
